TPU v7x, 256 devices: a whole 4x4x8 slice. The times are simulated.
256 devices in a mesh: blk: 32 (over y_lo, z, core), head: 8 (over x, y_hi).
Axes of the slice: x: 4, y: 4 (y_hi: 2, y_lo: 2; y = y_hi * 2 + y_lo), z: 8, core: 2. Of those that a mesh axis runs over, the one named last changes fastest.
Arguments:
- pages: bfloat16 [32, 16, 16, 768], P('blk'), may hold values from -6 to 6
- valid_counts: int32 [32], replicated, may hold values from 32 to 256
- dw_weight: float32 [7, 7, 768], replicated, may hold values from -0.875 to 0.875
- dw_bias: float32 [768], replicated, may hold values from -3 to 3
- norm1_gain: float32 [768], replicated, may hold values from 0.5 to 2
- fc1_w: bfloat16 [768, 3072], P(None, 'head'), may hold values from -0.21875 to 0.21875
- fc1_b: float32 [3072], P('head'), may hold values from -3 to 3
- fc2_w: bfloat16 [3072, 768], P('head'), may hold values from -0.109375 to 0.109375
- fc2_b: float32 [768], replicated, may hold values from -3 to 3
- layer_scale: float32 [768], replicated, may hold values from 0.5 to 2
- norm2_gain: float32 [768], replicated, may hold values from 0.5 to 2
- w_query: bfloat16 [768, 4096], P(None, 'head'), may hold values from -3 to 3
- w_key: bfloat16 [768, 1024], P(None, 'head'), may hold values from -0.21875 to 0.21875
- w_value: bfloat16 [768, 1024], P(None, 'head'), may hold values from -0.21875 to 0.21875
- w_out: bfloat16 [4096, 768], P('head'), may hold values from -0.09375 to 0.09375
Outputs:
- mixed: bfloat16 [8192, 768], P(('blk', 'head'))
All inputs are finite; a program needn't handle non-finite values.
Results may differ from a plain program's by a relative error of at most 0.023.
Values may be sent and summed in bfloat16 or wider, within the bound.
No kernel may reach another device: no remote copies, remote signals or barrier semaphores. Data moves between devices by JAX's collectives and lax.ppermute only.
A program may use at most 128 MiB of HBM per device.

v0:
```python
import jax
import jax.numpy as jnp
from jax import lax
from jax.sharding import PartitionSpec as P

HEADS = 32
KV_HEADS = 8
HD = 128


def depthwise(pages, dw_weight, dw_bias):
    height = pages.shape[1]
    breadth = pages.shape[2]
    padded = jnp.pad(pages.astype(jnp.float32), ((0, 0), (3, 3), (3, 3), (0, 0)))
    total = jnp.zeros(pages.shape, jnp.float32)
    for vertical in range(7):
        for sideways in range(7):
            total = (
                total
                + padded[:, vertical : vertical + height, sideways : sideways + breadth, :]
                * dw_weight[vertical, sideways]
            )
    return total + dw_bias


def layer_norm(values, gain, epsilon):
    centred = values - jnp.mean(values, axis=-1, keepdims=True)
    spread = jnp.mean(centred * centred, axis=-1, keepdims=True)
    return centred * lax.rsqrt(spread + epsilon) * gain


def mlp_partial(pages, dw_weight, dw_bias, norm1_gain, fc1_w, fc1_b, fc2_w):
    convolved = depthwise(pages, dw_weight, dw_bias)
    flattened = convolved.reshape(-1, convolved.shape[-1])
    normed = layer_norm(flattened, norm1_gain, 1e-06).astype(jnp.bfloat16)
    hidden = jax.nn.gelu(
        jnp.dot(normed, fc1_w, preferred_element_type=jnp.float32) + fc1_b, approximate=False
    ).astype(jnp.bfloat16)
    return jnp.dot(hidden, fc2_w, preferred_element_type=jnp.float32)


def fold_keys(carry, keys, values, queries, valid_counts, page_tokens):
    running_top, denominator, weighted = carry
    count = keys.shape[0]
    kv_groups = queries.shape[1]
    key_heads = keys.reshape(count, kv_groups, HD)
    value_heads = values.reshape(count, kv_groups, HD)
    scores = jnp.einsum(
        "rgqd,ngd->gqrn", queries, key_heads, preferred_element_type=jnp.float32
    ) * HD ** (-0.5)
    position = jnp.arange(count, dtype=jnp.int32)
    page_number = position // page_tokens
    matches = page_number[:, None] == jnp.arange(valid_counts.shape[0], dtype=jnp.int32)[None, :]
    page_count = jnp.sum(jnp.where(matches, valid_counts[None, :], 0), axis=1)
    valid = position % page_tokens < page_count
    scores = jnp.where(valid, scores, -1e30)
    new_top = jnp.maximum(running_top, jnp.max(scores, axis=-1))
    exponent = jnp.where(valid, jnp.exp(scores - new_top[..., None]), 0.0)
    denominator = jnp.sum(exponent, axis=-1)
    update = jnp.einsum(
        "gqrn,ngd->gqrd",
        exponent.astype(jnp.bfloat16),
        value_heads,
        preferred_element_type=jnp.float32,
    )
    weighted = update
    return (new_top, denominator, weighted)


def per_device(
    pages,
    valid_counts,
    dw_weight,
    dw_bias,
    norm1_gain,
    fc1_w,
    fc1_b,
    fc2_w,
    fc2_b,
    layer_scale,
    norm2_gain,
    w_query,
    w_key,
    w_value,
    w_out,
):
    channels = pages.shape[-1]
    page_tokens = pages.shape[1] * pages.shape[2]
    rows = pages.shape[0] * page_tokens
    partial_sum = mlp_partial(pages, dw_weight, dw_bias, norm1_gain, fc1_w, fc1_b, fc2_w)
    flat_pages = pages.reshape(rows, channels)
    summed = lax.psum(partial_sum, "head")
    block = flat_pages.astype(jnp.float32) + layer_scale * (summed + fc2_b)
    normed = layer_norm(block, norm2_gain, 1e-05).astype(jnp.bfloat16)
    kv_groups = w_key.shape[1] // HD
    group = HEADS // KV_HEADS
    queries = jnp.dot(normed, w_query, preferred_element_type=jnp.float32).astype(jnp.bfloat16)
    queries = queries.reshape(rows, kv_groups, group, HD)
    initial = (
        jnp.full((kv_groups, group, rows), -1e30, jnp.float32),
        jnp.zeros((kv_groups, group, rows), jnp.float32),
        jnp.zeros((kv_groups, group, rows, HD), jnp.float32),
    )
    own_keys = jnp.dot(normed, w_key, preferred_element_type=jnp.float32).astype(jnp.bfloat16)
    own_values = jnp.dot(normed, w_value, preferred_element_type=jnp.float32).astype(jnp.bfloat16)
    final = fold_keys(
        initial,
        lax.all_gather(own_keys, "blk", axis=0, tiled=True),
        lax.all_gather(own_values, "blk", axis=0, tiled=True),
        queries,
        valid_counts,
        page_tokens,
    )
    attended = (final[2] / final[1][..., None]).astype(jnp.bfloat16)
    attended = attended.transpose(2, 0, 1, 3).reshape(rows, kv_groups * group * HD)
    mixed = lax.psum_scatter(
        jnp.dot(attended, w_out, preferred_element_type=jnp.float32),
        "head",
        scatter_dimension=0,
        tiled=True,
    )
    return mixed.astype(jnp.bfloat16)


def solution(mesh):
    in_specs = (
        P("blk", None, None, None),
        P(),
        P(),
        P(),
        P(),
        P(None, "head"),
        P("head"),
        P("head", None),
        P(),
        P(),
        P(),
        P(None, "head"),
        P(None, "head"),
        P(None, "head"),
        P("head", None),
    )
    out_specs = P(("blk", "head"), None)
    return jax.shard_map(
        per_device, mesh=mesh, in_specs=in_specs, out_specs=out_specs, check_vma=False
    )
```

profile of v0, /device:TPU:2, one launch (start us, length us, event | category | flops | bytes accessed | tf_op | source)
XLA Modules:
  0.0 354.3 jit_solution(8926439461209473395)
XLA Ops:
  6.5 0.0 copy-start
  6.5 0.0 all-reduce.3.cloned.1.call-start
  6.5 1.3 slice_reduce_fusion.48
  7.9 1.4 slice_reduce_fusion.47
  9.3 1.1 slice_reduce_fusion.46
  10.4 1.1 convert_element_type.54
  11.5 7.0 %fusion.207 = (f32[16,16]{1,0:T(8,128)S(1)}, f32[1,16,16,768]{3,2,1,0:T(8,128)S(1)}) fusion(f32[768]{0:T(1024)} %param.18, f32[768]{0:T(1024)S(1)} %get-tuple-element.52, f32[768]{0:T(1024)S(1)} %get-tuple-element.53, f32[768]{0:T(1024)S(1)} %get-tuple-element.6, f32[768]{0:T(1024)S(1)} %get-tuple-element.7, f32[768]{0:T(1024)S(1)} %get-tuple-element.8, ...), kind=kLoop, calls=%fused_computation.328 | loop fusion | flops 19463936 | bytes 1727488 | tf_op jit(solution)/shard_map/reduce_sum | solution.py:27
  18.5 0.1 div.34
  18.6 0.2 multiply_reduce_fusion.1
  18.8 0.1 rsqrt.20
  18.9 0.9 fusion.122
  19.8 3.6 %fusion.133 = f32[256,768]{1,0:T(8,128)} fusion(bf16[384,768]{1,0:T(8,128)(2,1)} %param.22, bf16[256,768]{1,0:T(8,128)(2,1)S(1)} %fusion.122, bf16[768,384]{1,0:T(8,128)(2,1)} %param.20, f32[384]{0:T(512)} %param.21), kind=kOutput, calls=%fused_computation.195 | convolution fusion | flops 308477952 | bytes 2360832 | tf_op jit(solution)/shard_map/dot_general | solution.py:39
  23.4 0.0 all-reduce.3.cloned.1.call-update
  23.4 0.0 all-gather.3.cloned.1.call-start
  23.4 93.7 %all-reduce.3.cloned.1.call-done = f32[256,768]{1,0:T(8,128)} async-done(((f32[256,768]{1,0:T(8,128)}), f32[256,768]{1,0:T(8,128)}) %all-reduce.3.cloned.1.call-update) | async-done | bytes 786448 | tf_op jit(solution)/shard_map/psum | solution.py:92
  117.2 1.5 fusion.167
  118.6 1.5 multiply_reduce_fusion
  120.2 1.5 multiply_convert_fusion
  121.7 1.8 convolution_convert_fusion.2
  123.5 0.0 all-gather.3.cloned.1.call-update
  123.5 0.0 all-gather.5.cloned.1.call-start
  123.6 0.9 select_reduce_fusion
  124.5 1.5 fusion.12
  126.0 1.9 convolution_convert_fusion.1
  127.9 0.0 all-gather.5.cloned.1.call-update
  127.9 0.2 reduce-scatter.2.cloned.1.call-start
  128.1 59.5 %all-gather.3.cloned.1.call-done = bf16[8192,128]{1,0:T(8,128)(2,1)} async-done(((bf16[256,128]{1,0:T(8,128)(2,1)}), bf16[8192,128]{1,0:T(8,128)(2,1)}) %all-gather.3.cloned.1.call-update) | async-done | bytes 2097168 | tf_op jit(solution)/shard_map/all_gather | solution.py:108
  187.6 14.5 %bitcast_reduce_fusion = (f32[4,256]{1,0:T(4,128)S(1)}, f32[8192,256,4]{1,0,2:T(8,128)}) fusion(pred[8192]{0:T(1024)(128)(4,1)S(1)} %fusion.168, bf16[32,4,8,128]{3,2,1,0:T(8,128)(2,1)S(1)} %fusion.12, bf16[8192,128]{1,0:T(8,128)(2,1)} %all-gather.3.cloned.1.call-done), kind=kOutput, calls=%fused_computation.1 | convolution fusion | flops 2172648448 | bytes 35926016 | tf_op jit(solution)/shard_map/rgqd,ngd->gqrn/dot_general | solution.py:48
  202.1 15.1 %fusion.2 = f32[4,256]{1,0:T(4,128)S(1)} fusion(f32[8192,256,4]{1,0,2:T(8,128)} %get-tuple-element.57, f32[4,256]{1,0:T(4,128)S(1)} %broadcast_maximum_fusion, pred[8192]{0:T(1024)(128)(4,1)S(1)} %fusion.168), kind=kLoop, calls=%fused_computation.5 | loop fusion | flops 41942016 | bytes 33570816 | tf_op jit(solution)/shard_map/reduce_sum | solution.py:59
  217.3 38.0 %all-gather.5.cloned.1.call-done = bf16[8192,128]{0,1:T(8,128)(2,1)} async-done(((bf16[256,128]{0,1:T(8,128)(2,1)}), bf16[8192,128]{0,1:T(8,128)(2,1)}) %all-gather.5.cloned.1.call-update) | async-done | bytes 2097168 | tf_op jit(solution)/shard_map/all_gather | solution.py:109
  255.2 14.3 %fusion.18 = bf16[4,256,128]{1,2,0:T(8,128)(2,1)S(1)} fusion(f32[8192,256,4]{1,0,2:T(8,128)} %get-tuple-element.57, f32[4,256]{1,0:T(4,128)S(1)} %broadcast_maximum_fusion, pred[8192]{0:T(1024)(128)(4,1)S(1)} %fusion.168, bf16[8192,128]{0,1:T(8,128)(2,1)} %all-gather.5.cloned.1.call-done, f32[4,256]{1,0:T(4,128)S(1)} %fusion.2), kind=kOutput, calls=%fused_computation.70 | convolution fusion | flops 2189688832 | bytes 35930112 | tf_op jit(solution)/shard_map/gqrn,ngd->gqrd/dot_general | solution.py:60
  269.5 0.0 copy-done
  269.6 1.3 fusion.209
  270.8 0.0 reduce-scatter.2.cloned.1.call-update
  270.8 75.4 %reduce-scatter.2.cloned.1.call-done = f32[32,768]{1,0:T(8,128)} async-done(((f32[256,768]{1,0:T(8,128)}), f32[32,768]{1,0:T(8,128)}) %reduce-scatter.2.cloned.1.call-update) | async-done | bytes 98320 | tf_op jit(solution)/shard_map/reduce_scatter | solution.py:116
  346.2 1.5 convert_element_type.53
  (7 shorter events, 0.0 us)
Async XLA Ops:
  6.5 263.0 %copy-start = (bf16[512,768]{1,0:T(8,128)(2,1)S(1)}, bf16[512,768]{1,0:T(8,128)(2,1)}, u32[]{:S(2)}) copy-start(bf16[512,768]{1,0:T(8,128)(2,1)} %param.29) | copy-start | bytes 2359300
  6.5 110.6 %all-reduce.3.cloned.1.call-start = ((), (), s32[]{:S(2)}) async-start(), calls=%async_computation.1 | async-start | bytes 1572864 | tf_op jit(solution)/shard_map/psum | solution.py:92
  23.4 164.2 %all-gather.3.cloned.1.call-start = ((), (), s32[]{:S(2)}) async-start(), calls=%async_computation.2 | async-start | bytes 2162688 | tf_op jit(solution)/shard_map/all_gather | solution.py:108
  123.5 131.7 %all-gather.5.cloned.1.call-start = ((), (), s32[]{:S(2)}) async-start(), calls=%async_computation.3 | async-start | bytes 2162688 | tf_op jit(solution)/shard_map/all_gather | solution.py:109
  127.9 218.4 %reduce-scatter.2.cloned.1.call-start = ((), (), s32[]{:S(2)}) async-start(), calls=%async_computation.4 | async-start | bytes 884736 | tf_op jit(solution)/shard_map/reduce_scatter | solution.py:116
Sparse Core Ops, SparseCore 0:
  23.5 93.5 all-reduce.2
  123.6 63.9 all-gather.2
  189.5 65.6 all-gather.4
  271.0 75.2 reduce-scatter.1
where the time goes:
time: 355 us; the launch traced here: 354 us
  waiting for transfers between devices  267 us (75%)
  matrix products  38.8 us (11%)
  other arithmetic  31.2 us (9%)
  between operations  13.2 us (4%)
  local copies, waits for them, and re-layouts  4.04 us (1%)
    psum x1, waiting for transfers between devices, per_device(): summed = lax.psum(partial_sum, 'head')  93.7 us
    reduce_scatter x1, waiting for transfers between devices, per_device(): lax.psum_scatter(jnp.dot(attended, w_out, preferred_element_type=jnp.floa...  75.4 us
    all_gather x1, waiting for transfers between devices, per_device(): lax.all_gather(own_keys, 'blk', axis=0, tiled=True)  59.5 us
    all_gather x1, waiting for transfers between devices, per_device(): lax.all_gather(own_values, 'blk', axis=0, tiled=True)  38 us
    reduce_sum x1, other arithmetic, fold_keys(): denominator = jnp.sum(exponent, axis=-1)  15.1 us
    dot_general x1, matrix products, fold_keys(): jnp.einsum('rgqd,ngd->gqrn', queries, key_heads, preferred_element_type=j...  14.5 us
    dot_general x1, matrix products, fold_keys(): jnp.einsum('gqrn,ngd->gqrd', exponent.astype(jnp.bfloat16), value_heads,...  14.3 us
    reduce_sum x2, other arithmetic, layer_norm(): centred = values - jnp.mean(values, axis=-1, keepdims=True)  8.47 us
  transfers between devices with their start and end apart: 4, of which 4 were waited for; matrix products, arithmetic and copies ran while one was open for 10% of the time, Pallas kernels for 0%

commit v1 on v0

--- a/solution.py
+++ b/solution.py
@@ -6,6 +6,11 @@
 HEADS = 32
 KV_HEADS = 8
 HD = 128
+
+
+def swapped_in(shard, mesh_axis, along):
+    sent = jnp.stack([shard] * lax.axis_size(mesh_axis))
+    return jnp.concatenate(lax.all_to_all(sent, mesh_axis, 0, 0), axis=along)
 
 
 def depthwise(pages, dw_weight, dw_bias):
@@ -105,7 +110,7 @@
     own_values = jnp.dot(normed, w_value, preferred_element_type=jnp.float32).astype(jnp.bfloat16)
     final = fold_keys(
         initial,
-        lax.all_gather(own_keys, "blk", axis=0, tiled=True),
+        swapped_in(own_keys, "blk", 0),
         lax.all_gather(own_values, "blk", axis=0, tiled=True),
         queries,
         valid_counts,

time: 355 us -> 316 us (0.89)
  waiting for transfers between devices: 267 us -> 222 us
  starting transfers between devices: 0.31 us -> 7.69 us
    all_gather x1 -> x0, waiting for transfers between devices: 59.5 us -> none  [per_device(): lax.all_gather(own_keys, 'blk', axis=0, tiled=True)]
    all_to_all x0 -> x1, waiting for transfers between devices: none -> 50.6 us  [swapped_in(): return jnp.concatenate(lax.all_to_all(sent, mesh_axis, 0, 0), axis=along)]
    all_gather x1, waiting for transfers between devices: 38 us -> 1.41 us  [per_device(): lax.all_gather(own_values, 'blk', axis=0, tiled=True)]
    all_to_all x0 -> x1, starting transfers between devices: none -> 7.43 us  [swapped_in(): return jnp.concatenate(lax.all_to_all(sent, mesh_axis, 0, 0), axis=along)]
where the time goes in v1:
time: 316 us
  waiting for transfers between devices  222 us (70%)
  matrix products  35.7 us (11%)
  other arithmetic  31.2 us (10%)
  between operations  13.2 us (4%)
  starting transfers between devices  7.69 us (2%)
  local copies, waits for them, and re-layouts  5.9 us (2%)
    psum x1, waiting for transfers between devices, per_device(): summed = lax.psum(partial_sum, 'head')  93.7 us
    reduce_scatter x1, waiting for transfers between devices, per_device(): lax.psum_scatter(jnp.dot(attended, w_out, preferred_element_type=jnp.floa...  76 us
    all_to_all x1, waiting for transfers between devices, swapped_in(): return jnp.concatenate(lax.all_to_all(sent, mesh_axis, 0, 0), axis=along)  50.6 us
    reduce_sum x1, other arithmetic, fold_keys(): denominator = jnp.sum(exponent, axis=-1)  15.1 us
    dot_general x1, matrix products, fold_keys(): jnp.einsum('gqrn,ngd->gqrd', exponent.astype(jnp.bfloat16), value_heads,...  14.3 us
    dot_general x1, matrix products, fold_keys(): jnp.einsum('rgqd,ngd->gqrn', queries, key_heads, preferred_element_type=j...  12.1 us
    reduce_sum x2, other arithmetic, layer_norm(): centred = values - jnp.mean(values, axis=-1, keepdims=True)  8.47 us
    all_to_all x1, starting transfers between devices, swapped_in(): return jnp.concatenate(lax.all_to_all(sent, mesh_axis, 0, 0), axis=along)  7.43 us
  transfers between devices with their start and end apart: 4, of which 4 were waited for; matrix products, arithmetic and copies ran while one was open for 10% of the time, Pallas kernels for 0%

profile of v1, /device:TPU:2, one launch (start us, length us, event | category | flops | bytes accessed | tf_op | source)
XLA Modules:
  0.0 315.6 jit_solution(14187767594226010919)
XLA Ops:
  6.5 0.0 copy-start
  6.5 0.0 all-reduce.3.cloned.1.call-start
  6.5 1.4 slice_reduce_fusion.48
  7.9 1.4 slice_reduce_fusion.47
  9.3 1.1 slice_reduce_fusion.46
  10.4 1.1 convert_element_type.54
  11.5 7.0 %fusion.206 = (f32[16,16]{1,0:T(8,128)S(1)}, f32[1,16,16,768]{3,2,1,0:T(8,128)S(1)}) fusion(f32[768]{0:T(1024)} %param.18, f32[768]{0:T(1024)S(1)} %get-tuple-element.52, f32[768]{0:T(1024)S(1)} %get-tuple-element.53, f32[768]{0:T(1024)S(1)} %get-tuple-element.6, f32[768]{0:T(1024)S(1)} %get-tuple-element.7, f32[768]{0:T(1024)S(1)} %get-tuple-element.8, ...), kind=kLoop, calls=%fused_computation.327 | loop fusion | flops 19463936 | bytes 1727488 | tf_op jit(solution)/shard_map/reduce_sum | solution.py:32
  18.5 0.1 div.34
  18.6 0.2 multiply_reduce_fusion.1
  18.9 0.1 rsqrt.20
  18.9 0.9 fusion.120
  19.8 3.6 %fusion.131 = f32[256,768]{1,0:T(8,128)} fusion(bf16[384,768]{1,0:T(8,128)(2,1)} %param.22, bf16[256,768]{1,0:T(8,128)(2,1)S(1)} %fusion.120, bf16[768,384]{1,0:T(8,128)(2,1)} %param.20, f32[384]{0:T(512)} %param.21), kind=kOutput, calls=%fused_computation.193 | convolution fusion | flops 308477952 | bytes 2360832 | tf_op jit(solution)/shard_map/dot_general | solution.py:44
  23.4 0.0 all-reduce.3.cloned.1.call-update
  23.4 93.7 %all-reduce.3.cloned.1.call-done = f32[256,768]{1,0:T(8,128)} async-done(((f32[256,768]{1,0:T(8,128)}), f32[256,768]{1,0:T(8,128)}) %all-reduce.3.cloned.1.call-update) | async-done | bytes 786448 | tf_op jit(solution)/shard_map/psum | solution.py:97
  117.2 1.5 fusion.166
  118.6 1.5 multiply_reduce_fusion
  120.2 1.5 multiply_convert_fusion
  121.7 1.2 convolution_convert_fusion.2
  122.9 1.8 stack.2
  124.7 7.4 %all-to-all-start = ((bf16[32,256,128]{2,1,0:T(8,128)(2,1)}), bf16[32,256,128]{2,1,0:T(8,128)(2,1)S(1)}, u32[]{:S(2)}, u32[]{:S(2)}) async-start(bf16[32,256,128]{2,1,0:T(8,128)(2,1)} %stack.2), calls=%async_computation | async-start | bytes 4194304 | tf_op jit(solution)/shard_map/all_to_all | solution.py:13
  132.1 0.0 all-gather.2.cloned.1.call-start
  132.2 0.9 select_reduce_fusion
  133.1 1.8 convolution_convert_fusion.1
  134.9 0.0 all-gather.2.cloned.1.call-update
  135.0 0.2 reduce-scatter.2.cloned.1.call-start
  135.2 1.5 fusion.10
  136.7 50.6 %all-to-all-done = bf16[32,256,128]{2,1,0:T(8,128)(2,1)S(1)} async-done(((bf16[32,256,128]{2,1,0:T(8,128)(2,1)}), bf16[32,256,128]{2,1,0:T(8,128)(2,1)S(1)}, u32[]{:S(2)}, u32[]{:S(2)}) %all-to-all-start) | async-done | bytes 2097184 | tf_op jit(solution)/shard_map/all_to_all | solution.py:13
  187.3 12.1 %bitcast_reduce_fusion = (f32[4,256]{1,0:T(4,128)S(1)}, f32[8192,256,4]{1,0,2:T(8,128)}) fusion(pred[8192]{0:T(1024)(128)(4,1)S(1)} %fusion.167, bf16[8192,128,1]{1,0,2:T(8,128)(2,1)S(1)} %bitcast.92, bf16[32,4,8,128]{3,2,1,0:T(8,128)(2,1)S(1)} %fusion.10), kind=kOutput, calls=%fused_computation.1 | convolution fusion | flops 2172648448 | bytes 35926016 | tf_op jit(solution)/shard_map/rgqd,ngd->gqrn/dot_general | solution.py:53
  199.4 15.1 %fusion.2 = f32[4,256]{1,0:T(4,128)S(1)} fusion(f32[8192,256,4]{1,0,2:T(8,128)} %get-tuple-element.57, f32[4,256]{1,0:T(4,128)S(1)} %broadcast_maximum_fusion, pred[8192]{0:T(1024)(128)(4,1)S(1)} %fusion.167), kind=kLoop, calls=%fused_computation.5 | loop fusion | flops 41942016 | bytes 33570816 | tf_op jit(solution)/shard_map/reduce_sum | solution.py:64
  214.5 1.4 all-gather.2.cloned.1.call-done
  215.9 14.3 %fusion.16 = bf16[4,256,128]{1,2,0:T(8,128)(2,1)S(1)} fusion(f32[8192,256,4]{1,0,2:T(8,128)} %get-tuple-element.57, f32[4,256]{1,0:T(4,128)S(1)} %broadcast_maximum_fusion, pred[8192]{0:T(1024)(128)(4,1)S(1)} %fusion.167, bf16[8192,128]{0,1:T(8,128)(2,1)} %all-gather.2.cloned.1.call-done, f32[4,256]{1,0:T(4,128)S(1)} %fusion.2), kind=kOutput, calls=%fused_computation.68 | convolution fusion | flops 2189688832 | bytes 35930112 | tf_op jit(solution)/shard_map/gqrn,ngd->gqrd/dot_general | solution.py:65
  230.2 0.0 copy-done
  230.2 1.3 fusion.208
  231.5 0.0 reduce-scatter.2.cloned.1.call-update
  231.5 76.0 %reduce-scatter.2.cloned.1.call-done = f32[32,768]{1,0:T(8,128)} async-done(((f32[256,768]{1,0:T(8,128)}), f32[32,768]{1,0:T(8,128)}) %reduce-scatter.2.cloned.1.call-update) | async-done | bytes 98320 | tf_op jit(solution)/shard_map/reduce_scatter | solution.py:121
  307.5 1.5 convert_element_type.53
  (7 shorter events, 0.0 us)
Async XLA Ops:
  6.5 223.7 %copy-start = (bf16[512,768]{1,0:T(8,128)(2,1)S(1)}, bf16[512,768]{1,0:T(8,128)(2,1)}, u32[]{:S(2)}) copy-start(bf16[512,768]{1,0:T(8,128)(2,1)} %param.29) | copy-start | bytes 2359300
  6.5 110.6 %all-reduce.3.cloned.1.call-start = ((), (), s32[]{:S(2)}) async-start(), calls=%async_computation.2 | async-start | bytes 1572864 | tf_op jit(solution)/shard_map/psum | solution.py:97
  124.7 62.7 %all-to-all-start = ((bf16[32,256,128]{2,1,0:T(8,128)(2,1)}), bf16[32,256,128]{2,1,0:T(8,128)(2,1)S(1)}, u32[]{:S(2)}, u32[]{:S(2)}) async-start(bf16[32,256,128]{2,1,0:T(8,128)(2,1)} %stack.2), calls=%async_computation | async-start | bytes 4194304 | tf_op jit(solution)/shard_map/all_to_all | solution.py:13
  132.1 83.8 %all-gather.2.cloned.1.call-start = ((), (), s32[]{:S(2)}) async-start(), calls=%async_computation.3 | async-start | bytes 2162688 | tf_op jit(solution)/shard_map/all_gather | solution.py:114
  135.0 172.6 %reduce-scatter.2.cloned.1.call-start = ((), (), s32[]{:S(2)}) async-start(), calls=%async_computation.4 | async-start | bytes 884736 | tf_op jit(solution)/shard_map/reduce_scatter | solution.py:121
Sparse Core Ops, SparseCore 0:
  23.5 93.5 all-reduce.2
  135.1 80.8 all-gather.1
  231.6 75.8 reduce-scatter.1
